TPU v7x, 32 devices: a whole 2x2x4 slice. The times are simulated.
32 devices in a mesh: dp: 2 (over y), hid: 4 (over x, core), wid: 4 (over z).
Axes of the slice: x: 2, y: 2, z: 4, core: 2. Of those that a mesh axis runs over, the one named last changes fastest.
Arguments:
- hidden_in: bfloat16 [6144, 1536], P('dp', 'wid'), may hold values from -6 to 6
- cotangent: bfloat16 [6144, 1536], P('dp', 'wid'), may hold values from -6 to 6
- segments: int32 [8, 768], P(('dp', 'wid')), may hold values from 0 to 2, never falling along the last dimension, each value on 1 to 512 neighbouring positions
- gain_attn: bfloat16 [1536], P(('dp', 'wid')), may hold values from 0.5 to 1.5
- gain_mlp: bfloat16 [1536], P(('dp', 'wid')), may hold values from 0.5 to 1.5
- in_weight: bfloat16 [1536, 4, 1536], P(('dp', 'wid'), None, 'hid'), may hold values from -0.15625 to 0.15625
- beta_weight: bfloat16 [1536, 12], P(('dp', 'wid'), 'hid'), may hold values from -0.15625 to 0.15625
- out_weight: bfloat16 [1536, 1536], P('hid', ('dp', 'wid')), may hold values from -2.5 to 2.5
- gate_weight: bfloat16 [1536, 4096], P(('dp', 'wid'), 'hid'), may hold values from -0.15625 to 0.15625
- up_weight: bfloat16 [1536, 4096], P(('dp', 'wid'), 'hid'), may hold values from -0.15625 to 0.15625
- down_weight: bfloat16 [4096, 1536], P('hid', ('dp', 'wid')), may hold values from -0.1875 to 0.1875
Outputs:
- output: bfloat16 [6144, 1536], P('dp', 'wid')
- grad_input: float32 [6144, 1536], P('dp', 'wid')
- grad_gain_attn: float32 [1536], P(('dp', 'wid'))
- grad_gain_mlp: float32 [1536], P(('dp', 'wid'))
- grad_in_weight: float32 [1536, 4, 1536], P(('dp', 'wid'), None, 'hid')
- grad_beta_weight: float32 [1536, 12], P(('dp', 'wid'), 'hid')
- grad_out_weight: float32 [1536, 1536], P('hid', ('dp', 'wid'))
- grad_gate_weight: float32 [1536, 4096], P(('dp', 'wid'), 'hid')
- grad_up_weight: float32 [1536, 4096], P(('dp', 'wid'), 'hid')
- grad_down_weight: float32 [4096, 1536], P('hid', ('dp', 'wid'))
Inputs may be any that keep to these rules, and one draw needn't show every extreme that they name: `segments`: in each row (the 768 tokens of one block) ids never fall, each of the 3 ids occurs in one run of 1 to 512 tokens, and one run is exactly 512 long.
All inputs are finite; a program needn't handle non-finite values.
Results may differ from a plain program's by a relative error of at most 0.012.
The roundings to bfloat16 on the way count: a program that leaves them out, or rounds other values in their place, can miss the bound.
Values may be sent and summed in bfloat16 or wider, within the bound.
No kernel may reach another device: no remote copies, remote signals or barrier semaphores. Data moves between devices by JAX's collectives and lax.ppermute only.
A program may use at most 256 MiB of HBM per device.

v0:
```python
import jax
import jax.numpy as jnp
from jax import lax
from jax.sharding import PartitionSpec as P

HD = 128
BLK = 64


def householder_attention(
    queries, key_vecs, value_vecs, raw_dirs, beta_logit, segment_ids, block_size
):
    highest = lax.Precision.HIGHEST
    length, head_count, head_width = queries.shape
    block_count = length // block_size
    directions = raw_dirs * lax.rsqrt(jnp.sum(raw_dirs * raw_dirs, axis=-1, keepdims=True) + 1e-06)
    strengths = 2.0 * jax.nn.sigmoid(beta_logit)
    query_blocks = queries.reshape(block_count, block_size, head_count, head_width)
    key_blocks = key_vecs.reshape(block_count, block_size, head_count, head_width)
    dir_blocks = directions.reshape(block_count, block_size, head_count, head_width)
    strength_blocks = strengths.reshape(block_count, block_size, head_count).transpose(0, 2, 1)
    offsets = jnp.arange(block_size)
    strict_lower = (offsets[:, None] > offsets[None, :]).astype(jnp.float32)
    lower_incl = (offsets[:, None] >= offsets[None, :]).astype(jnp.float32)
    identity = jnp.eye(block_size, dtype=jnp.float32)
    gram_matrix = jnp.einsum("nshd,nthd->nhst", dir_blocks, dir_blocks, precision=highest)
    system = identity + strength_blocks[..., :, None] * gram_matrix * strict_lower
    right_side = identity * strength_blocks[..., :, None]
    tri_factor = jax.scipy.linalg.solve_triangular(
        system, right_side, lower=True, unit_diagonal=True
    )
    query_dirs = (
        jnp.einsum("nihd,nshd->nhis", query_blocks, dir_blocks, precision=highest) * lower_incl
    )
    dir_keys = (
        jnp.einsum("nthd,njhd->nhtj", dir_blocks, key_blocks, precision=highest) * strict_lower
    )
    factor_keys = jnp.einsum("nhst,nhtj->nhsj", tri_factor, dir_keys, precision=highest)
    inner_scores = jnp.einsum("nihd,njhd->nhij", query_blocks, key_blocks, precision=highest)
    inner_scores = inner_scores - jnp.einsum(
        "nhis,nhsj->nhij", query_dirs, factor_keys, precision=highest
    )
    keys_moved = key_blocks - jnp.einsum(
        "nhsj,nshd->njhd", factor_keys, dir_blocks, precision=highest
    )
    query_factor = jnp.einsum("nhis,nhst->nhit", query_dirs, tri_factor, precision=highest)
    queries_moved = query_blocks - jnp.einsum(
        "nhit,nthd->nihd", query_factor, dir_blocks, precision=highest
    )

    def sweep_step(moved_rows, item):
        block_index, keys_here, dirs_here, factor_here, inner_here, queries_here = item
        start = block_index * block_size
        zero_index = start * 0
        scores = jnp.einsum("ihd,jhd->hij", moved_rows, keys_here, precision=highest)
        scores = lax.dynamic_update_slice(scores, inner_here, (zero_index, start, zero_index))
        projected = jnp.einsum("ihd,shd->his", moved_rows, dirs_here, precision=highest)
        projected = jnp.einsum("his,hst->hit", projected, factor_here, precision=highest)
        moved_rows = moved_rows - jnp.einsum(
            "hit,thd->ihd", projected, dirs_here, precision=highest
        )
        moved_rows = lax.dynamic_update_slice(
            moved_rows, queries_here, (start, zero_index, zero_index)
        )
        return (moved_rows, scores)

    initial = jnp.zeros((length, head_count, head_width), jnp.float32)
    items = (
        jnp.arange(block_count, dtype=jnp.int32),
        keys_moved,
        dir_blocks,
        tri_factor,
        inner_scores,
        queries_moved,
    )
    _, scores = lax.scan(jax.checkpoint(sweep_step), initial, items, reverse=True)
    scores = scores.transpose(1, 2, 0, 3).reshape(head_count, length, length)
    position = jnp.arange(length)
    allowed = (position[None, :] <= position[:, None]) & (
        segment_ids[:, None] == segment_ids[None, :]
    )
    scores = jnp.where(allowed[None], scores * head_width ** (-0.5), -1e30)
    row_top = jnp.max(scores, axis=-1, keepdims=True)
    exponent = jnp.exp(scores - row_top)
    attn_probs = exponent / jnp.sum(exponent, axis=-1, keepdims=True)
    return jnp.einsum("hij,jhd->ihd", attn_probs, value_vecs, precision=highest)


def norm_back(values, scale_row, gain, grad_out):
    weighted = grad_out * gain
    grad_gain = jnp.sum(grad_out * values * scale_row, axis=0)
    grad_values = scale_row * weighted - values * scale_row**3 * jnp.mean(
        weighted * values, axis=-1, keepdims=True
    )
    return (grad_gain, grad_values)


def body(
    hidden_in,
    cotangent,
    segments,
    gain_attn,
    gain_mlp,
    in_weight,
    beta_weight,
    out_weight,
    gate_weight,
    up_weight,
    down_weight,
):
    highest = lax.Precision.HIGHEST
    token_in, token_grad = (
        lax.all_to_all(hidden_in, "wid", split_axis=0, concat_axis=1, tiled=True),
        lax.all_to_all(cotangent, "wid", split_axis=0, concat_axis=1, tiled=True),
    )
    gathered = (
        lax.all_gather(gain_attn, ("dp", "wid"), axis=0, tiled=True),
        lax.all_gather(gain_mlp, ("dp", "wid"), axis=0, tiled=True),
        lax.all_gather(in_weight, ("dp", "wid"), axis=0, tiled=True),
        lax.all_gather(beta_weight, ("dp", "wid"), axis=0, tiled=True),
        lax.all_gather(out_weight, ("dp", "wid"), axis=1, tiled=True),
        lax.all_gather(gate_weight, ("dp", "wid"), axis=0, tiled=True),
        lax.all_gather(up_weight, ("dp", "wid"), axis=0, tiled=True),
        lax.all_gather(down_weight, ("dp", "wid"), axis=1, tiled=True),
    )
    gain_one, gain_two, weight_in, weight_beta, weight_out, weight_gate, weight_up, weight_down = (
        gathered
    )
    gain_one = gain_one.astype(jnp.float32)
    gain_two = gain_two.astype(jnp.float32)
    row_count = token_in.shape[0]
    head_count = weight_beta.shape[1]
    seg_row = segments[0]
    inputs = token_in.astype(jnp.float32)
    scale_one = lax.rsqrt(jnp.mean(inputs * inputs, axis=-1, keepdims=True) + 1e-06)
    normed = (inputs * scale_one * gain_one).astype(jnp.bfloat16)
    projected = jnp.einsum(
        "td,dkc->tkc", normed, weight_in, preferred_element_type=jnp.float32
    ).astype(jnp.bfloat16)
    logits = jnp.dot(normed, weight_beta, preferred_element_type=jnp.float32)
    pieces = projected.astype(jnp.float32).reshape(row_count, 4, head_count, HD)
    query_in = pieces[:, 0]
    key_in = pieces[:, 1]
    value_in = pieces[:, 2]
    dirs_in = pieces[:, 3]

    def attend(queries, key_vecs, value_vecs, raw_dirs, beta_logit):
        return householder_attention(
            queries, key_vecs, value_vecs, raw_dirs, beta_logit, seg_row, BLK
        )

    attended = attend(query_in, key_in, value_in, dirs_in, logits)
    attended = attended.reshape(row_count, head_count * HD).astype(jnp.bfloat16)
    branch = lax.psum(jnp.dot(attended, weight_out, preferred_element_type=jnp.float32), "hid")
    middle = inputs + branch
    scale_two = lax.rsqrt(jnp.mean(middle * middle, axis=-1, keepdims=True) + 1e-06)
    mixed = (middle * scale_two * gain_two).astype(jnp.bfloat16)
    gate = jnp.dot(mixed, weight_gate, preferred_element_type=jnp.float32)
    upward = jnp.dot(mixed, weight_up, preferred_element_type=jnp.float32)
    sigmoid_gate = jax.nn.sigmoid(gate)
    silu_gate = gate * sigmoid_gate
    product = (silu_gate * upward).astype(jnp.bfloat16)
    feed = lax.psum(
        jnp.dot(product, weight_down, preferred_element_type=jnp.float32).astype(jnp.bfloat16),
        "hid",
    ).astype(jnp.float32)
    output = lax.all_to_all(
        (middle + feed).astype(jnp.bfloat16), "wid", split_axis=1, concat_axis=0, tiled=True
    )
    grad_product = jnp.einsum(
        "td,fd->tf", token_grad, weight_down, preferred_element_type=jnp.float32
    )
    grad_down = jnp.einsum("tf,td->fd", product, token_grad, preferred_element_type=jnp.float32)
    grad_gate_pre = (
        grad_product * upward * sigmoid_gate * (1.0 + gate * (1.0 - sigmoid_gate))
    ).astype(jnp.bfloat16)
    grad_up_pre = (grad_product * silu_gate).astype(jnp.bfloat16)
    grad_mixed_part = jnp.einsum(
        "tf,df->td", grad_gate_pre, weight_gate, preferred_element_type=jnp.float32
    )
    grad_mixed_part = grad_mixed_part + jnp.einsum(
        "tf,df->td", grad_up_pre, weight_up, preferred_element_type=jnp.float32
    )
    grad_gate = jnp.einsum("td,tf->df", mixed, grad_gate_pre, preferred_element_type=jnp.float32)
    grad_up = jnp.einsum("td,tf->df", mixed, grad_up_pre, preferred_element_type=jnp.float32)
    grad_mixed = lax.psum(grad_mixed_part, "hid")
    grad_gain_two, grad_middle = norm_back(middle, scale_two, gain_two, grad_mixed)
    grad_middle = grad_middle + token_grad.astype(jnp.float32)
    grad_branch = grad_middle.astype(jnp.bfloat16)
    grad_attended = jnp.einsum(
        "td,cd->tc", grad_branch, weight_out, preferred_element_type=jnp.float32
    )
    grad_out = jnp.einsum("tc,td->cd", attended, grad_branch, preferred_element_type=jnp.float32)
    grad_heads = grad_attended.reshape(row_count, head_count, HD)
    _, attend_again = jax.vjp(attend, query_in, key_in, value_in, dirs_in, logits)
    grads_attn = attend_again(grad_heads)
    grad_query, grad_key, grad_value, grad_dirs, grad_logit = grads_attn
    grad_proj = jnp.stack((grad_query, grad_key, grad_value, grad_dirs), axis=1)
    grad_proj = grad_proj.reshape(row_count, 4, head_count * HD).astype(jnp.bfloat16)
    grad_normed_part = jnp.einsum(
        "tkc,dkc->td", grad_proj, weight_in, preferred_element_type=jnp.float32
    )
    grad_normed_part = grad_normed_part + jnp.dot(
        grad_logit, weight_beta.astype(jnp.float32).T, precision=highest
    )
    grad_in = jnp.einsum("td,tkc->dkc", normed, grad_proj, preferred_element_type=jnp.float32)
    grad_beta = jnp.dot(normed.astype(jnp.float32).T, grad_logit, precision=highest)
    grad_normed = lax.psum(grad_normed_part, "hid")
    grad_gain_one, grad_inputs = norm_back(inputs, scale_one, gain_one, grad_normed)
    grad_inputs = grad_inputs + grad_middle
    grad_input = lax.all_to_all(grad_inputs, "wid", split_axis=1, concat_axis=0, tiled=True)
    shares = (
        lax.psum_scatter(grad_gain_one, ("dp", "wid"), scatter_dimension=0, tiled=True),
        lax.psum_scatter(grad_gain_two, ("dp", "wid"), scatter_dimension=0, tiled=True),
        lax.psum_scatter(grad_in, ("dp", "wid"), scatter_dimension=0, tiled=True),
        lax.psum_scatter(grad_beta, ("dp", "wid"), scatter_dimension=0, tiled=True),
        lax.psum_scatter(grad_out, ("dp", "wid"), scatter_dimension=1, tiled=True),
        lax.psum_scatter(grad_gate, ("dp", "wid"), scatter_dimension=0, tiled=True),
        lax.psum_scatter(grad_up, ("dp", "wid"), scatter_dimension=0, tiled=True),
        lax.psum_scatter(grad_down, ("dp", "wid"), scatter_dimension=1, tiled=True),
    )
    return (
        output,
        grad_input,
        shares[0],
        shares[1],
        shares[2],
        shares[3],
        shares[4],
        shares[5],
        shares[6],
        shares[7],
    )


def solution(mesh):
    placed = (
        P("dp", "wid"),
        P("dp", "wid"),
        P(("dp", "wid"), None),
        P(("dp", "wid")),
        P(("dp", "wid")),
        P(("dp", "wid"), None, "hid"),
        P(("dp", "wid"), "hid"),
        P("hid", ("dp", "wid")),
        P(("dp", "wid"), "hid"),
        P(("dp", "wid"), "hid"),
        P("hid", ("dp", "wid")),
    )
    return jax.shard_map(
        body,
        mesh=mesh,
        in_specs=placed,
        out_specs=(
            P("dp", "wid"),
            P("dp", "wid"),
            P(("dp", "wid")),
            P(("dp", "wid")),
            P(("dp", "wid"), None, "hid"),
            P(("dp", "wid"), "hid"),
            P("hid", ("dp", "wid")),
            P(("dp", "wid"), "hid"),
            P(("dp", "wid"), "hid"),
            P("hid", ("dp", "wid")),
        ),
        check_vma=False,
    )
```

profile of v0, /device:TPU:0, one launch (start us, length us, event | category | flops | bytes accessed | tf_op | source)
XLA Modules:
  0.0 2532.5 jit_solution(9748514839555380016)
XLA Ops:
  9.3 6.5 all-to-all-start
  18.4 89.2 %all-reduce.5 = (bf16[1536]{0:T(1024)(128)(2,1)S(1)}, bf16[1536]{0:T(1024)(128)(2,1)S(1)}) all-reduce(bf16[1536]{0:T(1024)(128)(2,1)S(1)} %dynamic-update-slice, bf16[1536]{0:T(1024)(128)(2,1)S(1)} %dynamic-update-slice.1), channel_id=1, replica_groups=mesh['dp'=2,'hid'=4,'wid'=4] {'dp','wid'}, use_global_device_ids=true, to_apply=%add | all-reduce | flops 3072 | bytes 12288
  107.6 27.1 %all-gather = bf16[8,192,3]{1,2,0:T(4,128)(2,1)S(1)} all-gather(bf16[1,192,3]{1,2,0:T(4,128)(2,1)S(1)} %bitcast.620), channel_id=1, replica_groups=mesh['dp'=2,'hid'=4,'wid'=4] {'dp','wid'}, dimensions={0}, use_global_device_ids=true | all-gather | bytes 10368 | tf_op jit(solution)/shard_map/all_gather | solution.py:120
  142.9 6.2 fusion.66
  158.4 177.1 %custom-call.8 = f32[12,3,1,64,64]{3,4,2,1,0:T(8,128)S(1)} custom-call(f32[12,3,1,64,64]{4,3,2,1,0:T(8,128)S(1)} %add_bitcast_fusion), custom_call_target="InvertDiagBlocksLowerTriangular" | custom-call | tf_op jit(solution)/shard_map/jit(_solve_triangular)/vmap(vmap())/triangular_solve/custom-call.1 | solution.py:29
  360.9 4.6 fusion.82
  372.6 6.7 broadcast_in_dim.127
  383.1 167.9 %while.59 = (s32[]{:T(128)}, f32[768,3,128]{0,2,1:T(8,128)S(1)}, f32[12,3,768,64]{2,3,1,0:T(8,128)}, f32[12,768,3,128]{1,3,2,0:T(8,128)}, f32[12,64,3,128]{3,1,2...) while((s32[]{:T(128)}, f32[768,3,128]{0,2,1:T(8,128)S(1)}, ...), condition=%wide.region_12.14_spmd.clone, body=%wide.region_11.13_spmd.sunk.clone | while | flops 793018368 | bytes 12189915 | solution.py:76
  554.8 155.0 %while.58 = (s32[]{:T(128)}, f32[768,3,128]{0,2,1:T(8,128)S(1)}, f32[12,3,768,64]{2,3,1,0:T(8,128)}, f32[12,64,3,128]{3,1,2,0:T(8,128)}, f32[12,3,64,64]{2,3,1,0...) while((s32[]{:T(128)}, f32[768,3,128]{0,2,1:T(8,128)S(1)}, ...), condition=%wide.region_3.5_spmd.clone, body=%wide.region_2.4_spmd.sunk.clone | while | flops 793018368 | bytes 9830607 | solution.py:76
  709.8 6.3 select_reduce_fusion.1
  730.0 5.0 fusion.167
  740.7 39.9 %all-to-all-done.2 = bf16[4,768,384]{2,1,0:T(8,128)(2,1)S(1)} async-done(((bf16[4,768,384]{2,1,0:T(8,128)(2,1)}), bf16[4,768,384]{2,1,0:T(8,128)(2,1)S(1)}, u32[]{:S(2)}, u32[]{:S(2)}) %all-to-all-start.2) | async-done | bytes 2359328 | tf_op jit(solution)/shard_map/all_to_all | solution.py:114
  783.9 43.4 %all-reduce.11.cloned.1.call-done = f32[768,1536]{1,0:T(8,128)} async-done(((f32[768,1536]{1,0:T(8,128)}), f32[768,1536]{1,0:T(8,128)}) %all-reduce.11.cloned.1.call-update) | async-done | bytes 4718608 | tf_op jit(solution)/shard_map/psum | solution.py:154
  835.7 54.2 %all-gather.11.cloned.1.call-done = bf16[1536,1024]{1,0:T(8,128)(2,1)} async-done(((bf16[192,1024]{1,0:T(8,128)(2,1)}), bf16[1536,1024]{1,0:T(8,128)(2,1)}) %all-gather.11.cloned.1.call-update) | async-done | bytes 3145744 | tf_op jit(solution)/shard_map/all_gather | solution.py:122
  889.9 6.9 fusion.168
  896.8 54.2 %all-gather.13.cloned.1.call-done = bf16[1536,1024]{1,0:T(8,128)(2,1)} async-done(((bf16[192,1024]{1,0:T(8,128)(2,1)}), bf16[1536,1024]{1,0:T(8,128)(2,1)}) %all-gather.13.cloned.1.call-update) | async-done | bytes 3145744 | tf_op jit(solution)/shard_map/all_gather | solution.py:123
  951.0 6.8 fusion.169
  957.8 54.2 %all-gather.15.cloned.1.call-done = bf16[1024,1536]{0,1:T(8,128)(2,1)} async-done(((bf16[1024,192]{0,1:T(8,128)(2,1)}), bf16[1024,1536]{0,1:T(8,128)(2,1)}) %all-gather.15.cloned.1.call-update) | async-done | bytes 3145744 | tf_op jit(solution)/shard_map/all_gather | solution.py:124
  1012.0 7.9 multiply_convert_fusion.2
  1023.0 4.5 convolution_add_fusion
  1028.8 5.7 convolution_convert_fusion
  1041.6 78.6 %all-reduce.15.cloned.1.call-done = f32[768,1536]{1,0:T(8,128)} async-done(((f32[768,1536]{1,0:T(8,128)}), f32[768,1536]{1,0:T(8,128)}) %all-reduce.15.cloned.1.call-update) | async-done | bytes 4718608 | tf_op jit(solution)/shard_map/psum | solution.py:186
  1120.2 5.7 multiply_reduce_fusion.1
  1125.9 52.5 %all-reduce.13.cloned.1.call-done = bf16[768,1536]{1,0:T(8,128)(2,1)} async-done(((bf16[768,1536]{1,0:T(8,128)(2,1)}), bf16[768,1536]{1,0:T(8,128)(2,1)}) %all-reduce.13.cloned.1.call-update) | async-done | bytes 2359312 | tf_op jit(solution)/shard_map/psum | solution.py:163
  1178.4 7.9 convert_add_fusion
  1188.4 9.1 subtract_exponential_fusion
  1207.2 388.8 %while.60 = (s32[]{:T(128)}, f32[768,3,128]{2,0,1:T(8,128)}, f32[12,64,3,128]{3,1,2,0:T(8,128)}, f32[12,64,3,128]{3,1,2,0:T(8,128)}, f32[12,3,64,64]{3,2,1,0:T(8...) while((s32[]{:T(128)}, f32[768,3,128]{2,0,1:T(8,128)}, ...), condition=%wide.region_19.21_spmd.clone.clone, body=%wide.region_18.20_spmd.clone.sunk.clone | while | flops 1926684672 | bytes 39472068 | solution.py:76
  1650.8 10.9 fusion.86
  1677.7 5.9 fusion.125
  1683.6 4.5 bitcast_add_fusion
  1694.0 7.7 fusion.60
  1702.8 5.3 fusion.103
  1709.8 6.0 fusion.173
  1715.8 6.2 fusion.174
  1723.7 6.0 fusion.175
  1733.0 4.8 all-to-all-start.1
  1737.8 44.6 %all-reduce.17.cloned.1.call-done = f32[768,1536]{1,0:T(8,128)} async-done(((f32[768,1536]{1,0:T(8,128)}), f32[768,1536]{1,0:T(8,128)}) %all-reduce.17.cloned.1.call-update) | async-done | bytes 4718608 | tf_op jit(solution)/shard_map/psum | solution.py:208
  1782.4 5.1 multiply_reduce_fusion.2
  1787.5 4.5 subtract_add_fusion
  1794.5 5.1 all-to-all-start.3
  1800.2 116.1 %reduce-scatter.19.cloned.1.call-done = f32[192,3]{1,0:T(8,128)} async-done(((f32[1536,3]{1,0:T(8,128)}), f32[192,3]{1,0:T(8,128)}) %reduce-scatter.19.cloned.1.call-update) | async-done | bytes 2320
  1917.9 36.1 %all-reduce.4 = (f32[1536]{0:T(1024)S(1)}, f32[1536]{0:T(1024)S(1)}) all-reduce(f32[1536]{0:T(1024)S(1)} %get-tuple-element.653, f32[1536]{0:T(1024)S(1)} %copy-done.83), channel_id=2, replica_groups=mesh['dp'=2,'hid'=4,'wid'=4] {'dp','wid'}, use_global_device_ids=true, to_apply=%region_26.29.clone | all-reduce | flops 3072 | bytes 24576
  1955.3 127.3 %reduce-scatter.9.cloned.1.call-done = f32[192,4,384]{2,0,1:T(8,128)} async-done(((f32[1536,4,384]{2,0,1:T(8,128)}), f32[192,4,384]{2,0,1:T(8,128)}) %reduce-scatter.9.cloned.1.call-update) | async-done | bytes 1179664 | tf_op jit(solution)/shard_map/reduce_scatter | solution.py:215
  2085.6 69.3 %reduce-scatter.11.cloned.1.call-done = f32[384,192]{0,1:T(8,128)} async-done(((f32[384,1536]{0,1:T(8,128)}), f32[384,192]{0,1:T(8,128)}) %reduce-scatter.11.cloned.1.call-update) | async-done | bytes 294928 | tf_op jit(solution)/shard_map/reduce_scatter | solution.py:217
  2154.9 121.6 %reduce-scatter.13.cloned.1.call-done = f32[192,1024]{1,0:T(8,128)} async-done(((f32[1536,1024]{1,0:T(8,128)}), f32[192,1024]{1,0:T(8,128)}) %reduce-scatter.13.cloned.1.call-update) | async-done | bytes 786448 | tf_op jit(solution)/shard_map/reduce_scatter | solution.py:218
  2276.5 121.5 %reduce-scatter.15.cloned.1.call-done = f32[192,1024]{1,0:T(8,128)} async-done(((f32[1536,1024]{1,0:T(8,128)}), f32[192,1024]{1,0:T(8,128)}) %reduce-scatter.15.cloned.1.call-update) | async-done | bytes 786448 | tf_op jit(solution)/shard_map/reduce_scatter | solution.py:219
  2398.0 121.6 %reduce-scatter.17.cloned.1.call-done = f32[1024,192]{0,1:T(8,128)} async-done(((f32[1024,1536]{0,1:T(8,128)}), f32[1024,192]{0,1:T(8,128)}) %reduce-scatter.17.cloned.1.call-update) | async-done | bytes 786448 | tf_op jit(solution)/shard_map/reduce_scatter | solution.py:220
  2521.0 4.8 copy.419
  (1059 shorter events, 893.3 us)
Async XLA Ops:
  7.2 135.7 %all-gather.7.cloned.1.call-start = ((), (), s32[]{:S(2)}) async-start(), calls=%async_computation.10 | async-start | bytes 5308416 | tf_op jit(solution)/shard_map/all_gather | solution.py:119
  9.2 7.3 copy-start.87
  9.2 8.6 copy-start.90
  9.2 8.9 copy-start.91
  9.2 98.3 %copy-start.86 = (bf16[192,3]{0,1:T(4,128)(2,1)S(1)}, bf16[192,3]{0,1:T(4,128)(2,1)}, u32[]{:S(2)}) copy-start(bf16[192,3]{0,1:T(4,128)(2,1)} %param.27) | copy-start | bytes 3460
  9.2 125.5 %copy-start.85 = (s32[1,768]{1,0:T(1,128)S(1)}, s32[1,768]{1,0:T(1,128)}, u32[]{:S(2)}) copy-start(s32[1,768]{1,0:T(1,128)} %param.23) | copy-start | bytes 9220
  9.3 128.9 %all-to-all-start = ((bf16[4,768,384]{2,1,0:T(8,128)(2,1)}), bf16[4,768,384]{2,1,0:T(8,128)(2,1)S(1)}, u32[]{:S(2)}, u32[]{:S(2)}) async-start(bf16[4,768,384]{2,1,0:T(8,128)(2,1)} %bitcast.612), calls=%async_computation | async-start | bytes 4718592 | tf_op jit(solution)/shard_map/all_to_all | solution.py:113
  15.7 714.3 %all-gather.9.cloned.1.call-start = ((), (), s32[]{:S(2)}) async-start(), calls=%async_computation.11 | async-start | bytes 1327104 | tf_op jit(solution)/shard_map/all_gather | solution.py:121
  16.5 810.9 %all-reduce.11.cloned.1.call-start = ((), (), s32[]{:S(2)}) async-start(), calls=%async_computation.12 | async-start | bytes 9437184 | tf_op jit(solution)/shard_map/psum | solution.py:154
  107.6 33.2 %copy-start.69 = (f32[1536]{0:T(1024)}, f32[1536]{0:T(1024)S(1)}, u32[]{:S(2)}) copy-start(f32[1536]{0:T(1024)S(1)} %convert_element_type.109) | copy-start | bytes 18436
  134.8 6.4 copy-start.72
  135.5 22.3 copy-start.58
  135.6 22.2 copy-start.65
  135.6 22.2 copy-start.79
  142.9 14.9 copy-start.61
  154.7 213.6 %copy-start = (f32[12,64,3,128]{3,1,0,2:T(8,128)}, f32[12,64,3,128]{3,1,0,2:T(8,128)S(1)}, u32[]{:S(2)}) copy-start(f32[12,64,3,128]{3,1,0,2:T(8,128)S(1)} %broadcast_multiply_fusion) | copy-start | bytes 3538948
  338.7 13.2 copy-start.10
  346.6 14.3 copy-start.14
  554.8 155.0 %copy-start.50 = (pred[768,12,64]{0,2,1:T(8,128)(4,1)S(1)}, pred[768,12,64]{0,2,1:T(8,128)(4,1)}, u32[]{:S(2)}) copy-start(pred[768,12,64]{0,2,1:T(8,128)(4,1)} %fusion.65) | copy-start | bytes 1769476
  709.8 6.4 slice-start.2
  709.8 7.2 slice-start.3
  709.8 9.2 copy-start.7
  735.1 154.8 %all-gather.11.cloned.1.call-start = ((), (), s32[]{:S(2)}) async-start(), calls=%async_computation.13 | async-start | bytes 3538944 | tf_op jit(solution)/shard_map/all_gather | solution.py:122
  735.7 215.3 %all-gather.13.cloned.1.call-start = ((), (), s32[]{:S(2)}) async-start(), calls=%async_computation.14 | async-start | bytes 3538944 | tf_op jit(solution)/shard_map/all_gather | solution.py:123
  736.2 44.3 %all-to-all-start.2 = ((bf16[4,768,384]{2,1,0:T(8,128)(2,1)}), bf16[4,768,384]{2,1,0:T(8,128)(2,1)S(1)}, u32[]{:S(2)}, u32[]{:S(2)}) async-start(bf16[4,768,384]{2,1,0:T(8,128)(2,1)} %bitcast.613), calls=%async_computation.2 | async-start | bytes 4718592 | tf_op jit(solution)/shard_map/all_to_all | solution.py:114
  740.0 272.0 %all-gather.15.cloned.1.call-start = ((), (), s32[]{:S(2)}) async-start(), calls=%async_computation.15 | async-start | bytes 3538944 | tf_op jit(solution)/shard_map/all_gather | solution.py:124
  740.6 379.6 %all-reduce.15.cloned.1.call-start = ((), (), s32[]{:S(2)}) async-start(), calls=%async_computation.17 | async-start | bytes 9437184 | tf_op jit(solution)/shard_map/psum | solution.py:186
  783.9 228.1 %copy-start.44 = (bf16[4,96,8,384]{3,2,0,1:T(8,128)(2,1)}, bf16[4,96,8,384]{3,2,0,1:T(8,128)(2,1)S(1)}, u32[]{:S(2)}) copy-start(bf16[4,96,8,384]{3,2,0,1:T(8,128)(2,1)S(1)} %copy.300) | copy-start | bytes 7077892
  1012.0 7.9 copy-start.88
  1027.4 151.0 %all-reduce.13.cloned.1.call-start = ((), (), s32[]{:S(2)}) async-start(), calls=%async_computation.16 | async-start | bytes 4718592 | tf_op jit(solution)/shard_map/psum | solution.py:163
  1034.6 747.8 %all-reduce.17.cloned.1.call-start = ((), (), s32[]{:S(2)}) async-start(), calls=%async_computation.18 | async-start | bytes 9437184 | tf_op jit(solution)/shard_map/psum | solution.py:208
  1120.2 68.2 %slice-start = ((s8[7077888]{0:T(1024)(128)(4,1)}), s8[2883584]{0:T(1024)(128)(4,1)S(1)}, s32[]{:S(2)}) async-start(s8[7077888]{0:T(1024)(128)(4,1)} %bitcast.575), calls=%async_computation.25 | async-start | bytes 5767168
  1178.4 7.9 copy-start.56
  1178.4 10.0 slice-start.1
  1188.4 9.1 copy-start.51
  1207.2 388.9 %copy-start.1 = (f32[12,64,3,128]{3,1,0,2:T(8,128)S(1)}, f32[12,64,3,128]{3,1,0,2:T(8,128)}, u32[]{:S(2)}) copy-start(f32[12,64,3,128]{3,1,0,2:T(8,128)} %copy-done) | copy-start | bytes 3538948
  1688.1 228.2 %reduce-scatter.19.cloned.1.call-start = ((), (), s32[]{:S(2)}) async-start(), calls=%async_computation.24 | async-start | bytes 884736
  1693.9 388.6 %reduce-scatter.9.cloned.1.call-start = ((), (), s32[]{:S(2)}) async-start(), calls=%async_computation.19 | async-start | bytes 10616832 | tf_op jit(solution)/shard_map/reduce_scatter | solution.py:215
  1701.8 453.2 %reduce-scatter.11.cloned.1.call-start = ((), (), s32[]{:S(2)}) async-start(), calls=%async_computation.20 | async-start | bytes 2654208 | tf_op jit(solution)/shard_map/reduce_scatter | solution.py:217
  1708.1 568.4 %reduce-scatter.13.cloned.1.call-start = ((), (), s32[]{:S(2)}) async-start(), calls=%async_computation.21 | async-start | bytes 7077888 | tf_op jit(solution)/shard_map/reduce_scatter | solution.py:218
  1715.8 682.2 %reduce-scatter.15.cloned.1.call-start = ((), (), s32[]{:S(2)}) async-start(), calls=%async_computation.22 | async-start | bytes 7077888 | tf_op jit(solution)/shard_map/reduce_scatter | solution.py:219
  1722.1 797.5 %reduce-scatter.17.cloned.1.call-start = ((), (), s32[]{:S(2)}) async-start(), calls=%async_computation.23 | async-start | bytes 7077888 | tf_op jit(solution)/shard_map/reduce_scatter | solution.py:220
  1733.0 49.4 %copy-start.70 = (f32[1536]{0:T(1024)S(1)}, f32[1536]{0:T(1024)}, u32[]{:S(2)}) copy-start(f32[1536]{0:T(1024)} %copy-done.69) | copy-start | bytes 18436
  1733.0 49.4 %copy-start.82 = (f32[768]{0:T(1024)S(1)}, f32[768]{0:T(1024)}, u32[]{:S(2)}) copy-start(f32[768]{0:T(1024)} %copy-done.81) | copy-start | bytes 9220
  1733.0 61.5 %all-to-all-start.1 = ((bf16[768,4,384]{2,0,1:T(8,128)(2,1)}), bf16[768,4,384]{2,0,1:T(8,128)(2,1)S(1)}, u32[]{:S(2)}, u32[]{:S(2)}) async-start(bf16[768,4,384]{2,0,1:T(8,128)(2,1)} %bitcast.603), calls=%async_computation.1 | async-start | bytes 4718592 | tf_op jit(solution)/shard_map/all_to_all | solution.py:167
  1737.8 49.7 %copy-start.84 = (f32[768]{0:T(1024)S(1)}, f32[768]{0:T(1024)}, u32[]{:S(2)}) copy-start(f32[768]{0:T(1024)} %get-tuple-element.744) | copy-start | bytes 9220
  1794.5 123.4 %copy-start.83 = (f32[1536]{0:T(1024)S(1)}, f32[1536]{0:T(1024)}, u32[]{:S(2)}) copy-start(f32[1536]{0:T(1024)} %get-tuple-element.651) | copy-start | bytes 18436
  1794.5 160.8 %all-to-all-start.3 = ((f32[768,4,384]{2,0,1:T(8,128)}), f32[768,4,384]{2,0,1:T(8,128)}, u32[]{:S(2)}, u32[]{:S(2)}) async-start(f32[768,4,384]{2,0,1:T(8,128)} %bitcast.585), calls=%async_computation.3 | async-start | bytes 9437184 | tf_op jit(solution)/shard_map/all_to_all | solution.py:211
  (158 other events, 364.4 us)
Sparse Core Ops, SparseCore 0:
  10.7 117.8 all-gather.6
  130.7 40.6 all-gather.8
  735.2 92.0 all-reduce.10
  829.3 60.6 all-gather.10
  891.9 59.0 all-gather.12
  952.9 59.0 all-gather.14
  1027.6 92.6 all-reduce.14
  1122.6 55.7 all-reduce.12
  1688.2 94.0 all-reduce.16
  1786.1 130.1 reduce-scatter.18
  1920.3 162.1 reduce-scatter.8
  2086.9 68.0 reduce-scatter.10
  2159.5 116.9 reduce-scatter.12
  2280.9 117.0 reduce-scatter.14
  2402.4 117.0 reduce-scatter.16
where the time goes:
time: 2550 us; the launch traced here: 2530 us
  waiting for transfers between devices  1100 us (43%)
  matrix products  573 us (22%)
  local copies, waits for them, and re-layouts  387 us (15%)
  other arithmetic  255 us (10%)
  blocking collectives  152 us (6%)
  loops' own time  27.4 us (1%)
    another operation x6, other arithmetic, householder_attention(): jax.scipy.linalg.solve_triangular(system, right_side, lower=True, unit_di...  178 us
    reduce_scatter x1, waiting for transfers between devices, body(): lax.psum_scatter(grad_in, ('dp', 'wid'), scatter_dimension=0, tiled=True)  127 us
    unnamed x2, blocking collectives  125 us
    reduce_scatter x1, waiting for transfers between devices, body(): lax.psum_scatter(grad_gate, ('dp', 'wid'), scatter_dimension=0, tiled=True)  122 us
    reduce_scatter x1, waiting for transfers between devices, body(): lax.psum_scatter(grad_down, ('dp', 'wid'), scatter_dimension=1, tiled=True)  122 us
    reduce_scatter x1, waiting for transfers between devices, body(): lax.psum_scatter(grad_up, ('dp', 'wid'), scatter_dimension=0, tiled=True)  122 us
    unnamed x16, waiting for transfers between devices  119 us
    dot_general x48, matrix products, sweep_step(): jnp.einsum('ihd,jhd->hij', moved_rows, keys_here, precision=highest)  107 us
  transfers between devices with their start and end apart: 19, of which 14 were waited for; matrix products, arithmetic and copies ran while one was open for 26% of the time, Pallas kernels for 0%

commit v1 on v0

--- a/solution.py
+++ b/solution.py
@@ -2,6 +2,7 @@
 import jax.numpy as jnp
 from jax import lax
 from jax.sharding import PartitionSpec as P
+from jax.lax import all_gather
 
 HD = 128
 BLK = 64
@@ -183,7 +184,7 @@
     )
     grad_gate = jnp.einsum("td,tf->df", mixed, grad_gate_pre, preferred_element_type=jnp.float32)
     grad_up = jnp.einsum("td,tf->df", mixed, grad_up_pre, preferred_element_type=jnp.float32)
-    grad_mixed = lax.psum(grad_mixed_part, "hid")
+    grad_mixed = jnp.sum(all_gather(grad_mixed_part, axis_name="hid"), axis=0)
     grad_gain_two, grad_middle = norm_back(middle, scale_two, gain_two, grad_mixed)
     grad_middle = grad_middle + token_grad.astype(jnp.float32)
     grad_branch = grad_middle.astype(jnp.bfloat16)

time: 2550 us -> 2580 us (1.012)
    all_gather x0 -> x1, waiting for transfers between devices: none -> 102 us  [body(): grad_mixed = jnp.sum(all_gather(grad_mixed_part, axis_name='hid'), axis=0)]
    psum x1 -> x0, waiting for transfers between devices: 78.6 us -> none  [body(): grad_mixed = lax.psum(grad_mixed_part, 'hid')]
  transfers between devices with their start and end apart: 19 -> 19, of which waited for: 14 -> 14; matrix products, arithmetic and copies ran while one was open for 26% -> 27% of each run, Pallas kernels for 0% -> 0%
where the time goes in v1:
time: 2580 us; the launch traced here: 2560 us
  waiting for transfers between devices  1110 us (43%)
  matrix products  572 us (22%)
  local copies, waits for them, and re-layouts  387 us (15%)
  other arithmetic  267 us (10%)
  blocking collectives  153 us (6%)
  loops' own time  27.4 us (1%)
    another operation x6, other arithmetic, householder_attention(): jax.scipy.linalg.solve_triangular(system, right_side, lower=True, unit_di...  178 us
    reduce_scatter x1, waiting for transfers between devices, body(): lax.psum_scatter(grad_in, ('dp', 'wid'), scatter_dimension=0, tiled=True)  127 us
    unnamed x2, blocking collectives  125 us
    reduce_scatter x1, waiting for transfers between devices, body(): lax.psum_scatter(grad_up, ('dp', 'wid'), scatter_dimension=0, tiled=True)  122 us
    reduce_scatter x1, waiting for transfers between devices, body(): lax.psum_scatter(grad_down, ('dp', 'wid'), scatter_dimension=1, tiled=True)  122 us
    reduce_scatter x1, waiting for transfers between devices, body(): lax.psum_scatter(grad_gate, ('dp', 'wid'), scatter_dimension=0, tiled=True)  118 us
    unnamed x16, waiting for transfers between devices  113 us
    dot_general x48, matrix products, sweep_step(): jnp.einsum('ihd,jhd->hij', moved_rows, keys_here, precision=highest)  107 us
  transfers between devices with their start and end apart: 19, of which 14 were waited for; matrix products, arithmetic and copies ran while one was open for 27% of the time, Pallas kernels for 0%

profile of v1, /device:TPU:0, one launch (start us, length us, event | category | flops | bytes accessed | tf_op | source)
XLA Modules:
  0.0 2558.2 jit_solution(9289017855896606336)
XLA Ops:
  9.3 6.5 all-to-all-start
  18.3 89.2 %all-reduce.5 = (bf16[1536]{0:T(1024)(128)(2,1)S(1)}, bf16[1536]{0:T(1024)(128)(2,1)S(1)}) all-reduce(bf16[1536]{0:T(1024)(128)(2,1)S(1)} %dynamic-update-slice, bf16[1536]{0:T(1024)(128)(2,1)S(1)} %dynamic-update-slice.1), channel_id=1, replica_groups=mesh['dp'=2,'hid'=4,'wid'=4] {'dp','wid'}, use_global_device_ids=true, to_apply=%add | all-reduce | flops 3072 | bytes 12288
  107.6 27.1 %all-gather.1 = bf16[8,192,3]{1,2,0:T(4,128)(2,1)S(1)} all-gather(bf16[1,192,3]{1,2,0:T(4,128)(2,1)S(1)} %bitcast.622), channel_id=1, replica_groups=mesh['dp'=2,'hid'=4,'wid'=4] {'dp','wid'}, dimensions={0}, use_global_device_ids=true | all-gather | bytes 10368 | tf_op jit(solution)/shard_map/all_gather | solution.py:121
  142.8 6.2 fusion.66
  158.3 177.1 %custom-call.8 = f32[12,3,1,64,64]{3,4,2,1,0:T(8,128)S(1)} custom-call(f32[12,3,1,64,64]{4,3,2,1,0:T(8,128)S(1)} %add_bitcast_fusion), custom_call_target="InvertDiagBlocksLowerTriangular" | custom-call | tf_op jit(solution)/shard_map/jit(_solve_triangular)/vmap(vmap())/triangular_solve/custom-call.1 | solution.py:30
  360.9 4.6 fusion.82
  372.6 6.7 broadcast_in_dim.127
  383.0 167.9 %while.59 = (s32[]{:T(128)}, f32[768,3,128]{0,2,1:T(8,128)S(1)}, f32[12,3,768,64]{2,3,1,0:T(8,128)}, f32[12,768,3,128]{1,3,2,0:T(8,128)}, f32[12,64,3,128]{3,1,2...) while((s32[]{:T(128)}, f32[768,3,128]{0,2,1:T(8,128)S(1)}, ...), condition=%wide.region_12.14_spmd.clone, body=%wide.region_11.13_spmd.sunk.clone | while | flops 793018368 | bytes 12189915 | solution.py:77
  554.7 154.9 %while.58 = (s32[]{:T(128)}, f32[768,3,128]{0,2,1:T(8,128)S(1)}, f32[12,3,768,64]{2,3,1,0:T(8,128)}, f32[12,64,3,128]{3,1,2,0:T(8,128)}, f32[12,3,64,64]{2,3,1,0...) while((s32[]{:T(128)}, f32[768,3,128]{0,2,1:T(8,128)S(1)}, ...), condition=%wide.region_3.5_spmd.clone, body=%wide.region_2.4_spmd.sunk.clone | while | flops 793018368 | bytes 9830607 | solution.py:77
  709.6 6.3 select_reduce_fusion.1
  729.8 5.1 fusion.167
  740.6 39.9 %all-to-all-done.2 = bf16[4,768,384]{2,1,0:T(8,128)(2,1)S(1)} async-done(((bf16[4,768,384]{2,1,0:T(8,128)(2,1)}), bf16[4,768,384]{2,1,0:T(8,128)(2,1)S(1)}, u32[]{:S(2)}, u32[]{:S(2)}) %all-to-all-start.2) | async-done | bytes 2359328 | tf_op jit(solution)/shard_map/all_to_all | solution.py:115
  783.8 43.4 %all-reduce.10.cloned.1.call-done = f32[768,1536]{1,0:T(8,128)} async-done(((f32[768,1536]{1,0:T(8,128)}), f32[768,1536]{1,0:T(8,128)}) %all-reduce.10.cloned.1.call-update) | async-done | bytes 4718608 | tf_op jit(solution)/shard_map/psum | solution.py:155
  835.6 54.2 %all-gather.13.cloned.1.call-done = bf16[1536,1024]{1,0:T(8,128)(2,1)} async-done(((bf16[192,1024]{1,0:T(8,128)(2,1)}), bf16[1536,1024]{1,0:T(8,128)(2,1)}) %all-gather.13.cloned.1.call-update) | async-done | bytes 3145744 | tf_op jit(solution)/shard_map/all_gather | solution.py:123
  889.8 6.8 fusion.168
  896.7 54.2 %all-gather.15.cloned.1.call-done = bf16[1536,1024]{1,0:T(8,128)(2,1)} async-done(((bf16[192,1024]{1,0:T(8,128)(2,1)}), bf16[1536,1024]{1,0:T(8,128)(2,1)}) %all-gather.15.cloned.1.call-update) | async-done | bytes 3145744 | tf_op jit(solution)/shard_map/all_gather | solution.py:124
  950.9 6.8 fusion.169
  957.7 54.2 %all-gather.17.cloned.1.call-done = bf16[1024,1536]{0,1:T(8,128)(2,1)} async-done(((bf16[1024,192]{0,1:T(8,128)(2,1)}), bf16[1024,1536]{0,1:T(8,128)(2,1)}) %all-gather.17.cloned.1.call-update) | async-done | bytes 3145744 | tf_op jit(solution)/shard_map/all_gather | solution.py:125
  1011.9 7.9 multiply_convert_fusion.2
  1028.7 5.8 convolution_convert_fusion
  1034.5 5.0 multiply_bitcast_fusion
  1039.5 5.0 copy.201
  1044.6 101.6 %all-gather.19.cloned.1.call-done = f32[3072,1536]{1,0:T(8,128)} async-done(((f32[768,1536]{1,0:T(8,128)}), f32[3072,1536]{1,0:T(8,128)}) %all-gather.19.cloned.1.call-update) | async-done | bytes 18874384 | tf_op jit(solution)/shard_map/all_gather | solution.py:187
  1146.1 11.3 reduce_sum.147
  1157.4 5.8 multiply_reduce_fusion.1
  1163.2 41.0 %all-reduce.12.cloned.1.call-done = bf16[768,1536]{1,0:T(8,128)(2,1)} async-done(((bf16[768,1536]{1,0:T(8,128)(2,1)}), bf16[768,1536]{1,0:T(8,128)(2,1)}) %all-reduce.12.cloned.1.call-update) | async-done | bytes 2359312 | tf_op jit(solution)/shard_map/psum | solution.py:164
  1204.2 7.9 convert_add_fusion
  1214.3 9.0 subtract_exponential_fusion
  1233.1 388.5 %while.60 = (s32[]{:T(128)}, f32[768,3,128]{2,0,1:T(8,128)}, f32[12,64,3,128]{3,1,2,0:T(8,128)}, f32[12,64,3,128]{3,1,2,0:T(8,128)}, f32[12,3,64,64]{3,2,1,0:T(8...) while((s32[]{:T(128)}, f32[768,3,128]{2,0,1:T(8,128)}, ...), condition=%wide.region_19.21_spmd.clone.clone, body=%wide.region_18.20_spmd.clone.sunk.clone | while | flops 1926684672 | bytes 39472068 | solution.py:77
  1676.3 10.9 fusion.86
  1703.2 5.9 fusion.125
  1719.5 7.8 fusion.60
  1728.9 6.0 fusion.173
  1734.9 6.0 fusion.174
  1742.7 6.2 fusion.175
  1752.2 4.7 all-to-all-start.1
  1756.9 51.0 %all-reduce.14.cloned.1.call-done = f32[768,1536]{1,0:T(8,128)} async-done(((f32[768,1536]{1,0:T(8,128)}), f32[768,1536]{1,0:T(8,128)}) %all-reduce.14.cloned.1.call-update) | async-done | bytes 4718608 | tf_op jit(solution)/shard_map/psum | solution.py:209
  1807.9 5.1 multiply_reduce_fusion.2
  1819.9 5.1 all-to-all-start.3
  1825.1 5.2 fusion.103
  1830.9 110.9 %reduce-scatter.19.cloned.1.call-done = f32[192,3]{1,0:T(8,128)} async-done(((f32[1536,3]{1,0:T(8,128)}), f32[192,3]{1,0:T(8,128)}) %reduce-scatter.19.cloned.1.call-update) | async-done | bytes 2320
  1943.4 36.2 %all-reduce.4 = (f32[1536]{0:T(1024)S(1)}, f32[1536]{0:T(1024)S(1)}) all-reduce(f32[1536]{0:T(1024)S(1)} %get-tuple-element.653, f32[1536]{0:T(1024)S(1)} %copy-done.83), channel_id=3, replica_groups=mesh['dp'=2,'hid'=4,'wid'=4] {'dp','wid'}, use_global_device_ids=true, to_apply=%region_26.29.clone | all-reduce | flops 3072 | bytes 24576
  1980.9 127.2 %reduce-scatter.9.cloned.1.call-done = f32[192,4,384]{2,0,1:T(8,128)} async-done(((f32[1536,4,384]{2,0,1:T(8,128)}), f32[192,4,384]{2,0,1:T(8,128)}) %reduce-scatter.9.cloned.1.call-update) | async-done | bytes 1179664 | tf_op jit(solution)/shard_map/reduce_scatter | solution.py:216
  2111.1 118.4 %reduce-scatter.13.cloned.1.call-done = f32[192,1024]{1,0:T(8,128)} async-done(((f32[1536,1024]{1,0:T(8,128)}), f32[192,1024]{1,0:T(8,128)}) %reduce-scatter.13.cloned.1.call-update) | async-done | bytes 786448 | tf_op jit(solution)/shard_map/reduce_scatter | solution.py:219
  2229.5 121.7 %reduce-scatter.15.cloned.1.call-done = f32[192,1024]{1,0:T(8,128)} async-done(((f32[1536,1024]{1,0:T(8,128)}), f32[192,1024]{1,0:T(8,128)}) %reduce-scatter.15.cloned.1.call-update) | async-done | bytes 786448 | tf_op jit(solution)/shard_map/reduce_scatter | solution.py:220
  2351.2 121.6 %reduce-scatter.17.cloned.1.call-done = f32[1024,192]{0,1:T(8,128)} async-done(((f32[1024,1536]{0,1:T(8,128)}), f32[1024,192]{0,1:T(8,128)}) %reduce-scatter.17.cloned.1.call-update) | async-done | bytes 786448 | tf_op jit(solution)/shard_map/reduce_scatter | solution.py:221
  2472.8 72.4 %reduce-scatter.11.cloned.1.call-done = f32[384,192]{0,1:T(8,128)} async-done(((f32[384,1536]{0,1:T(8,128)}), f32[384,192]{0,1:T(8,128)}) %reduce-scatter.11.cloned.1.call-update) | async-done | bytes 294928 | tf_op jit(solution)/shard_map/reduce_scatter | solution.py:218
  2546.6 4.8 copy.420
  (1060 shorter events, 898.4 us)
Async XLA Ops:
  7.2 135.6 %all-gather.9.cloned.1.call-start = ((), (), s32[]{:S(2)}) async-start(), calls=%async_computation.10 | async-start | bytes 5308416 | tf_op jit(solution)/shard_map/all_gather | solution.py:120
  9.2 7.3 copy-start.87
  9.2 8.6 copy-start.90
  9.2 8.8 copy-start.91
  9.2 98.3 %copy-start.86 = (bf16[192,3]{0,1:T(4,128)(2,1)S(1)}, bf16[192,3]{0,1:T(4,128)(2,1)}, u32[]{:S(2)}) copy-start(bf16[192,3]{0,1:T(4,128)(2,1)} %param.27) | copy-start | bytes 3460
  9.2 125.5 %copy-start.85 = (s32[1,768]{1,0:T(1,128)S(1)}, s32[1,768]{1,0:T(1,128)}, u32[]{:S(2)}) copy-start(s32[1,768]{1,0:T(1,128)} %param.23) | copy-start | bytes 9220
  9.3 128.9 %all-to-all-start = ((bf16[4,768,384]{2,1,0:T(8,128)(2,1)}), bf16[4,768,384]{2,1,0:T(8,128)(2,1)S(1)}, u32[]{:S(2)}, u32[]{:S(2)}) async-start(bf16[4,768,384]{2,1,0:T(8,128)(2,1)} %bitcast.614), calls=%async_computation | async-start | bytes 4718592 | tf_op jit(solution)/shard_map/all_to_all | solution.py:114
  15.7 714.1 %all-gather.11.cloned.1.call-start = ((), (), s32[]{:S(2)}) async-start(), calls=%async_computation.11 | async-start | bytes 1327104 | tf_op jit(solution)/shard_map/all_gather | solution.py:122
  16.5 810.8 %all-reduce.10.cloned.1.call-start = ((), (), s32[]{:S(2)}) async-start(), calls=%async_computation.12 | async-start | bytes 9437184 | tf_op jit(solution)/shard_map/psum | solution.py:155
  107.6 33.1 %copy-start.69 = (f32[1536]{0:T(1024)}, f32[1536]{0:T(1024)S(1)}, u32[]{:S(2)}) copy-start(f32[1536]{0:T(1024)S(1)} %convert_element_type.109) | copy-start | bytes 18436
  134.8 6.4 copy-start.72
  135.5 22.2 copy-start.58
  135.6 22.1 copy-start.65
  135.6 22.1 copy-start.79
  142.8 14.9 copy-start.61
  154.6 213.7 %copy-start = (f32[12,64,3,128]{3,1,0,2:T(8,128)}, f32[12,64,3,128]{3,1,0,2:T(8,128)S(1)}, u32[]{:S(2)}) copy-start(f32[12,64,3,128]{3,1,0,2:T(8,128)S(1)} %broadcast_multiply_fusion) | copy-start | bytes 3538948
  338.6 13.3 copy-start.10
  346.5 14.3 copy-start.14
  554.7 154.9 %copy-start.50 = (pred[768,12,64]{0,2,1:T(8,128)(4,1)S(1)}, pred[768,12,64]{0,2,1:T(8,128)(4,1)}, u32[]{:S(2)}) copy-start(pred[768,12,64]{0,2,1:T(8,128)(4,1)} %fusion.65) | copy-start | bytes 1769476
  709.6 6.4 slice-start.2
  709.6 7.2 slice-start.3
  709.6 9.2 copy-start.7
  735.0 154.8 %all-gather.13.cloned.1.call-start = ((), (), s32[]{:S(2)}) async-start(), calls=%async_computation.13 | async-start | bytes 3538944 | tf_op jit(solution)/shard_map/all_gather | solution.py:123
  735.6 215.3 %all-gather.15.cloned.1.call-start = ((), (), s32[]{:S(2)}) async-start(), calls=%async_computation.14 | async-start | bytes 3538944 | tf_op jit(solution)/shard_map/all_gather | solution.py:124
  736.2 44.3 %all-to-all-start.2 = ((bf16[4,768,384]{2,1,0:T(8,128)(2,1)}), bf16[4,768,384]{2,1,0:T(8,128)(2,1)S(1)}, u32[]{:S(2)}, u32[]{:S(2)}) async-start(bf16[4,768,384]{2,1,0:T(8,128)(2,1)} %bitcast.615), calls=%async_computation.2 | async-start | bytes 4718592 | tf_op jit(solution)/shard_map/all_to_all | solution.py:115
  739.9 272.0 %all-gather.17.cloned.1.call-start = ((), (), s32[]{:S(2)}) async-start(), calls=%async_computation.15 | async-start | bytes 3538944 | tf_op jit(solution)/shard_map/all_gather | solution.py:125
  740.5 405.6 %all-gather.19.cloned.1.call-start = ((), (), s32[]{:S(2)}) async-start(), calls=%async_computation.23 | async-start | bytes 23592960 | tf_op jit(solution)/shard_map/all_gather | solution.py:187
  783.8 228.1 %copy-start.44 = (bf16[4,96,8,384]{3,2,0,1:T(8,128)(2,1)}, bf16[4,96,8,384]{3,2,0,1:T(8,128)(2,1)S(1)}, u32[]{:S(2)}) copy-start(bf16[4,96,8,384]{3,2,0,1:T(8,128)(2,1)S(1)} %copy.301) | copy-start | bytes 7077892
  1011.9 7.9 copy-start.88
  1027.3 176.8 %all-reduce.12.cloned.1.call-start = ((), (), s32[]{:S(2)}) async-start(), calls=%async_computation.16 | async-start | bytes 4718592 | tf_op jit(solution)/shard_map/psum | solution.py:164
  1034.5 773.4 %all-reduce.14.cloned.1.call-start = ((), (), s32[]{:S(2)}) async-start(), calls=%async_computation.17 | async-start | bytes 9437184 | tf_op jit(solution)/shard_map/psum | solution.py:209
  1157.4 56.9 %slice-start = ((s8[7077888]{0:T(1024)(128)(4,1)}), s8[2883584]{0:T(1024)(128)(4,1)S(1)}, s32[]{:S(2)}) async-start(s8[7077888]{0:T(1024)(128)(4,1)} %bitcast.576), calls=%async_computation.25 | async-start | bytes 5767168
  1204.2 7.9 copy-start.56
  1204.2 10.1 slice-start.1
  1214.3 9.1 copy-start.51
  1233.1 388.5 %copy-start.1 = (f32[12,64,3,128]{3,1,0,2:T(8,128)S(1)}, f32[12,64,3,128]{3,1,0,2:T(8,128)}, u32[]{:S(2)}) copy-start(f32[12,64,3,128]{3,1,0,2:T(8,128)} %copy-done) | copy-start | bytes 3538948
  1713.6 228.2 %reduce-scatter.19.cloned.1.call-start = ((), (), s32[]{:S(2)}) async-start(), calls=%async_computation.24 | async-start | bytes 884736
  1719.4 388.6 %reduce-scatter.9.cloned.1.call-start = ((), (), s32[]{:S(2)}) async-start(), calls=%async_computation.18 | async-start | bytes 10616832 | tf_op jit(solution)/shard_map/reduce_scatter | solution.py:216
  1727.2 502.3 %reduce-scatter.13.cloned.1.call-start = ((), (), s32[]{:S(2)}) async-start(), calls=%async_computation.20 | async-start | bytes 7077888 | tf_op jit(solution)/shard_map/reduce_scatter | solution.py:219
  1734.9 616.3 %reduce-scatter.15.cloned.1.call-start = ((), (), s32[]{:S(2)}) async-start(), calls=%async_computation.21 | async-start | bytes 7077888 | tf_op jit(solution)/shard_map/reduce_scatter | solution.py:220
  1741.0 731.8 %reduce-scatter.17.cloned.1.call-start = ((), (), s32[]{:S(2)}) async-start(), calls=%async_computation.22 | async-start | bytes 7077888 | tf_op jit(solution)/shard_map/reduce_scatter | solution.py:221
  1752.2 55.7 %copy-start.70 = (f32[1536]{0:T(1024)S(1)}, f32[1536]{0:T(1024)}, u32[]{:S(2)}) copy-start(f32[1536]{0:T(1024)} %copy-done.69) | copy-start | bytes 18436
  1752.2 55.7 %copy-start.82 = (f32[768]{0:T(1024)S(1)}, f32[768]{0:T(1024)}, u32[]{:S(2)}) copy-start(f32[768]{0:T(1024)} %copy-done.81) | copy-start | bytes 9220
  1752.2 67.8 %all-to-all-start.1 = ((bf16[768,4,384]{2,0,1:T(8,128)(2,1)}), bf16[768,4,384]{2,0,1:T(8,128)(2,1)S(1)}, u32[]{:S(2)}, u32[]{:S(2)}) async-start(bf16[768,4,384]{2,0,1:T(8,128)(2,1)} %bitcast.605), calls=%async_computation.1 | async-start | bytes 4718592 | tf_op jit(solution)/shard_map/all_to_all | solution.py:168
  1756.9 56.1 %copy-start.84 = (f32[768]{0:T(1024)S(1)}, f32[768]{0:T(1024)}, u32[]{:S(2)}) copy-start(f32[768]{0:T(1024)} %get-tuple-element.744) | copy-start | bytes 9220
  1819.9 160.9 %all-to-all-start.3 = ((f32[768,4,384]{2,0,1:T(8,128)}), f32[768,4,384]{2,0,1:T(8,128)}, u32[]{:S(2)}, u32[]{:S(2)}) async-start(f32[768,4,384]{2,0,1:T(8,128)} %bitcast.587), calls=%async_computation.3 | async-start | bytes 9437184 | tf_op jit(solution)/shard_map/all_to_all | solution.py:212
  1825.1 720.1 %reduce-scatter.11.cloned.1.call-start = ((), (), s32[]{:S(2)}) async-start(), calls=%async_computation.19 | async-start | bytes 2654208 | tf_op jit(solution)/shard_map/reduce_scatter | solution.py:218
  1830.3 113.0 %copy-start.83 = (f32[1536]{0:T(1024)S(1)}, f32[1536]{0:T(1024)}, u32[]{:S(2)}) copy-start(f32[1536]{0:T(1024)} %get-tuple-element.651) | copy-start | bytes 18436
  (158 other events, 368.9 us)
Sparse Core Ops, SparseCore 0:
  10.7 117.8 all-gather.8
  130.7 40.5 all-gather.10
  735.1 92.0 all-reduce.9
  829.2 60.6 all-gather.12
  891.8 59.0 all-gather.14
  952.8 59.0 all-gather.16
  1027.4 118.6 all-gather.18
  1148.5 55.6 all-reduce.11
  1713.7 94.0 all-reduce.13
  1811.6 130.1 reduce-scatter.18
  1945.8 162.1 reduce-scatter.8
  2112.5 116.9 reduce-scatter.12
  2234.1 117.0 reduce-scatter.14
  2355.6 117.0 reduce-scatter.16
  2477.1 68.0 reduce-scatter.10
